TPU v7x, 32 devices: a whole 2x2x4 slice. The times are simulated.
32 devices in a mesh: tm: 2 (over x), slope: 4 (over y, core), act: 4 (over z).
Axes of the slice: x: 2, y: 2, z: 4, core: 2. Of those that a mesh axis runs over, the one named last changes fastest.
Arguments:
- frames: bfloat16 [16384, 1024], P('tm', 'slope'), may hold values from -6 to 6
- frame_scale: float32 [16384], P('tm'), may hold values from 0.5 to 2
- codes: int32 [16384], P('act'), may hold values from 0 to 16383, each once
- assign: int32 [1024], replicated, may hold values from 0 to 2
- loads: float32 [3], replicated, may hold values from 0.3 to 3
Outputs:
- gram_panel: float32 [16384, 1024], P('act')
- factor: float32 [1024, 1024], P('act')
Inputs may be any that keep to these rules, and one draw needn't show every extreme that they name: `codes`: each actuator has its own Hadamard row.
All inputs are finite; a program needn't handle non-finite values.
Results may differ from a plain program's by a relative error of at most 0.0055.
Values may be sent and summed in bfloat16 or wider, within the bound.
No kernel may reach another device: no remote copies, remote signals or barrier semaphores. Data moves between devices by JAX's collectives and lax.ppermute only.
A program may use at most 128 MiB of HBM per device.

v0:
```python
import math

import jax
import jax.numpy as jnp
from jax import lax
from jax.sharding import PartitionSpec as P

PW = 1024
NDM = 3


def broadcast(x, axis, root):
    mine = lax.axis_index(axis) == root
    return lax.psum(jnp.where(mine, x, jnp.zeros_like(x)), axis)


def parity_bits(values):
    folded = values
    for shift_by in (16, 8, 4, 2, 1):
        folded = jnp.bitwise_xor(folded, jnp.right_shift(folded, shift_by))
    return jnp.bitwise_and(folded, 1)


def contract_rows(left, right):
    return lax.dot_general(
        left, right, (((0,), (0,)), ((), ())), preferred_element_type=jnp.float32
    )


def exact_dot(left, right):
    return jnp.dot(left, right, precision=lax.Precision.HIGHEST, preferred_element_type=jnp.float32)


def local(frames, frame_scale, codes, assign, loads):
    f_dev = frames.shape[0]
    s_dev = frames.shape[1]
    a_dev = codes.shape[0]
    n_tm = lax.axis_size("tm")
    n_act = lax.axis_size("act")
    total_frames = f_dev * n_tm
    half_rows = s_dev // n_tm
    total_rows = half_rows * n_tm * lax.axis_size("slope")
    block = PW // n_act
    tm_pos = lax.axis_index("tm")
    act_pos = lax.axis_index("act")
    frame_ids = tm_pos * f_dev + lax.broadcasted_iota(jnp.int32, (f_dev, a_dev), 0)
    parity = parity_bits(jnp.bitwise_and(frame_ids, codes[None, :]))
    weights = ((1 - 2 * parity).astype(jnp.float32) * frame_scale[:, None]).astype(jnp.bfloat16)
    summed = lax.psum_scatter(contract_rows(frames, weights), "tm", scatter_dimension=0, tiled=True)
    im_rows = (summed * (1.0 / math.sqrt(total_frames))).astype(jnp.bfloat16)
    panel = broadcast(im_rows[:, :PW], "act", 0)
    gram_part = contract_rows(im_rows, panel)
    diag_part = contract_rows(lax.dynamic_slice_in_dim(panel, act_pos * block, block, 1), panel)
    gram_total, diag_total = lax.psum((gram_part, diag_part), ("tm", "slope"))
    gram_panel = gram_total / float(total_rows)
    mirror_ids = lax.broadcasted_iota(jnp.int32, (NDM, PW), 0)
    load_col = jnp.sum(jnp.where(assign[None, :] == mirror_ids, loads[:, None], 0.0), axis=0)
    row_ids = act_pos * block + lax.broadcasted_iota(jnp.int32, (block, PW), 0)
    col_ids = lax.broadcasted_iota(jnp.int32, (block, PW), 1)
    own_rows = diag_total / float(total_rows) + jnp.where(
        row_ids == col_ids, load_col[None, :], 0.0
    )
    identity = jnp.eye(block, dtype=jnp.float32)

    def step(k, lower_rows):
        offset = k * block
        target = lax.dynamic_slice_in_dim(own_rows, offset, block, 1)
        schur = target - exact_dot(lower_rows, lower_rows.T)
        diag_factor = jnp.linalg.cholesky(jnp.where(act_pos == k, schur, identity))
        placed = lax.dynamic_update_slice_in_dim(lower_rows, diag_factor, offset, 1)
        lower_rows = jnp.where(act_pos == k, placed, lower_rows)
        finished = broadcast(lower_rows, "act", k)
        pivot = lax.dynamic_slice_in_dim(finished, offset, block, 1)
        rest = target - exact_dot(lower_rows, finished.T)
        solved = lax.linalg.triangular_solve(
            pivot, rest, left_side=False, lower=True, transpose_a=True
        )
        updated = lax.dynamic_update_slice_in_dim(lower_rows, solved, offset, 1)
        return jnp.where(act_pos > k, updated, lower_rows)

    factor = lax.fori_loop(0, n_act, step, jnp.zeros((block, PW), jnp.float32))
    return (gram_panel, factor)


def solution(mesh):
    return jax.shard_map(
        local,
        mesh=mesh,
        in_specs=(P("tm", "slope"), P("tm"), P("act"), P(), P()),
        out_specs=(P("act", None), P("act", None)),
        check_vma=False,
    )
```

profile of v0, /device:TPU:0, one launch (start us, length us, event | category | flops | bytes accessed | tf_op | source)
XLA Modules:
  0.0 925.2 jit_solution(9085216612536026638)
XLA Ops:
  7.2 80.6 %fusion.20 = f32[256,4096]{0,1:T(8,128)} fusion(bf16[8192,256]{1,0:T(8,128)(2,1)} %param.7, f32[8192]{0:T(1024)} %param.8, s32[4096]{0:T(1024)} %param.9, s32[8192]{0:T(1024)S(1)} %iota_add_fusion), kind=kOutput, calls=%fused_computation.50 | convolution fusion | flops 17750294528 | bytes 8470528 | tf_op jit(solution)/shard_map/dot_general | solution.py:25
  88.0 57.1 %reduce-scatter.2.cloned.1.call-done = f32[128,4096]{0,1:T(8,128)} async-done(((f32[256,4096]{0,1:T(8,128)}), f32[128,4096]{0,1:T(8,128)}) %reduce-scatter.2.cloned.1.call-update) | async-done | bytes 2097168 | tf_op jit(solution)/shard_map/reduce_scatter | solution.py:49
  147.8 35.6 %all-reduce.6.cloned.1.call-done = bf16[128,1024]{0,1:T(8,128)(2,1)} async-done(((bf16[128,1024]{0,1:T(8,128)(2,1)}), bf16[128,1024]{0,1:T(8,128)(2,1)}) %all-reduce.6.cloned.1.call-update) | async-done | bytes 262160 | tf_op jit(solution)/shard_map/psum | solution.py:14
  194.4 229.1 %all-reduce.8.cloned.1.call-done = (f32[4096,1024]{1,0:T(8,128)}, f32[256,1024]{1,0:T(8,128)}) async-done(((f32[4096,1024]{1,0:T(8,128)}, f32[256,1024]{1,0:T(8,128)}), (f32[4096,1024]{1,0:T(8,128)}, f32[256,1024]{1,0:T(8,128)})) %all-reduce.8.cloned.1.call-update) | async-done | bytes 17825808 | tf_op jit(solution)/shard_map/psum | solution.py:54
  425.0 479.6 %while.18 = (s32[]{:T(128)}, f32[256,1024]{0,1:T(8,128)S(1)}, s32[]{:T(128)}, f32[256,1024]{1,0:T(8,128)S(1)}, s32[]{:T(128)}, /*index=5*/s32[]{:T(128)}, s32[]{...) while((s32[]{:T(128)}, f32[256,1024]{0,1:T(8,128)S(1)}, s32[]{:T(128)}, ...), condition=%wide.region_11.12_spmd.clone, body=%wide.region_5.11_spmd.clone.sunk | while | flops 1813627136 | bytes 20318660 | solution.py:81
  427.3 11.7 %cholesky.222 = f32[128,128]{1,0:T(8,128)S(1)} custom-call(f32[128,128]{1,0:T(8,128)S(1)} %cholesky.221), custom_call_target="Cholesky" | custom-call | tf_op jit(solution)/shard_map/while/body/eval_jaxpr/jit(cholesky)/cholesky | solution.py:69
  439.1 9.8 %custom-call.36 = f32[1,128,128]{1,2,0:T(8,128)S(1)} custom-call(f32[1,128,128]{2,1,0:T(8,128)S(1)} %get-tuple-element.221), custom_call_target="InvertDiagBlocksLowerTriangular" | custom-call | tf_op jit(solution)/shard_map/while/body/eval_jaxpr/jit(cholesky)/cholesky | solution.py:69
  449.3 11.7 %cholesky.224 = f32[128,128]{1,0:T(8,128)S(1)} custom-call(f32[128,128]{1,0:T(8,128)S(1)} %convolution_subtract_fusion.7), custom_call_target="Cholesky" | custom-call | tf_op jit(solution)/shard_map/while/body/eval_jaxpr/jit(cholesky)/cholesky | solution.py:69
  464.5 51.9 %all-reduce.10.cloned.1.call-done = f32[256,1024]{0,1:T(8,128)} async-done(((f32[256,1024]{0,1:T(8,128)}), f32[256,1024]{0,1:T(8,128)}) %all-reduce.10.cloned.1.call-update) | async-done | bytes 1048592 | tf_op jit(solution)/shard_map/while/body/eval_jaxpr/psum | solution.py:14
  521.6 19.7 %custom-call.38 = f32[2,128,128]{1,2,0:T(8,128)S(1)} custom-call(f32[2,128,128]{2,1,0:T(8,128)S(1)} %get-tuple-element.225), custom_call_target="InvertDiagBlocksLowerTriangular" | custom-call | tf_op jit(solution)/shard_map/while/body/eval_jaxpr/triangular_solve | solution.py:75
  547.7 11.7 %cholesky.222 = f32[128,128]{1,0:T(8,128)S(1)} custom-call(f32[128,128]{1,0:T(8,128)S(1)} %cholesky.221), custom_call_target="Cholesky" | custom-call | tf_op jit(solution)/shard_map/while/body/eval_jaxpr/jit(cholesky)/cholesky | solution.py:69
  569.7 11.7 %cholesky.224 = f32[128,128]{1,0:T(8,128)S(1)} custom-call(f32[128,128]{1,0:T(8,128)S(1)} %convolution_subtract_fusion.7), custom_call_target="Cholesky" | custom-call | tf_op jit(solution)/shard_map/while/body/eval_jaxpr/jit(cholesky)/cholesky | solution.py:69
  584.8 51.3 %all-reduce.10.cloned.1.call-done = f32[256,1024]{0,1:T(8,128)} async-done(((f32[256,1024]{0,1:T(8,128)}), f32[256,1024]{0,1:T(8,128)}) %all-reduce.10.cloned.1.call-update) | async-done | bytes 1048592 | tf_op jit(solution)/shard_map/while/body/eval_jaxpr/psum | solution.py:14
  641.4 19.7 %custom-call.38 = f32[2,128,128]{1,2,0:T(8,128)S(1)} custom-call(f32[2,128,128]{2,1,0:T(8,128)S(1)} %get-tuple-element.225), custom_call_target="InvertDiagBlocksLowerTriangular" | custom-call | tf_op jit(solution)/shard_map/while/body/eval_jaxpr/triangular_solve | solution.py:75
  667.4 11.7 %cholesky.222 = f32[128,128]{1,0:T(8,128)S(1)} custom-call(f32[128,128]{1,0:T(8,128)S(1)} %cholesky.221), custom_call_target="Cholesky" | custom-call | tf_op jit(solution)/shard_map/while/body/eval_jaxpr/jit(cholesky)/cholesky | solution.py:69
  679.2 9.8 %custom-call.36 = f32[1,128,128]{1,2,0:T(8,128)S(1)} custom-call(f32[1,128,128]{2,1,0:T(8,128)S(1)} %get-tuple-element.221), custom_call_target="InvertDiagBlocksLowerTriangular" | custom-call | tf_op jit(solution)/shard_map/while/body/eval_jaxpr/jit(cholesky)/cholesky | solution.py:69
  689.5 11.7 %cholesky.224 = f32[128,128]{1,0:T(8,128)S(1)} custom-call(f32[128,128]{1,0:T(8,128)S(1)} %convolution_subtract_fusion.7), custom_call_target="Cholesky" | custom-call | tf_op jit(solution)/shard_map/while/body/eval_jaxpr/jit(cholesky)/cholesky | solution.py:69
  704.6 51.3 %all-reduce.10.cloned.1.call-done = f32[256,1024]{0,1:T(8,128)} async-done(((f32[256,1024]{0,1:T(8,128)}), f32[256,1024]{0,1:T(8,128)}) %all-reduce.10.cloned.1.call-update) | async-done | bytes 1048592 | tf_op jit(solution)/shard_map/while/body/eval_jaxpr/psum | solution.py:14
  761.1 19.7 %custom-call.38 = f32[2,128,128]{1,2,0:T(8,128)S(1)} custom-call(f32[2,128,128]{2,1,0:T(8,128)S(1)} %get-tuple-element.225), custom_call_target="InvertDiagBlocksLowerTriangular" | custom-call | tf_op jit(solution)/shard_map/while/body/eval_jaxpr/triangular_solve | solution.py:75
  787.2 11.7 %cholesky.222 = f32[128,128]{1,0:T(8,128)S(1)} custom-call(f32[128,128]{1,0:T(8,128)S(1)} %cholesky.221), custom_call_target="Cholesky" | custom-call | tf_op jit(solution)/shard_map/while/body/eval_jaxpr/jit(cholesky)/cholesky | solution.py:69
  809.2 11.7 %cholesky.224 = f32[128,128]{1,0:T(8,128)S(1)} custom-call(f32[128,128]{1,0:T(8,128)S(1)} %convolution_subtract_fusion.7), custom_call_target="Cholesky" | custom-call | tf_op jit(solution)/shard_map/while/body/eval_jaxpr/jit(cholesky)/cholesky | solution.py:69
  824.3 51.3 %all-reduce.10.cloned.1.call-done = f32[256,1024]{0,1:T(8,128)} async-done(((f32[256,1024]{0,1:T(8,128)}), f32[256,1024]{0,1:T(8,128)}) %all-reduce.10.cloned.1.call-update) | async-done | bytes 1048592 | tf_op jit(solution)/shard_map/while/body/eval_jaxpr/psum | solution.py:14
  880.9 19.7 %custom-call.38 = f32[2,128,128]{1,2,0:T(8,128)S(1)} custom-call(f32[2,128,128]{2,1,0:T(8,128)S(1)} %get-tuple-element.225), custom_call_target="InvertDiagBlocksLowerTriangular" | custom-call | tf_op jit(solution)/shard_map/while/body/eval_jaxpr/triangular_solve | solution.py:75
  906.0 12.4 %broadcast_multiply_fusion = f32[4096,1024]{1,0:T(8,128)} fusion(f32[4096,1024]{1,0:T(8,128)} %get-tuple-element.152), kind=kLoop, calls=%fused_computation.49 | loop fusion | flops 4194304 | bytes 33554432 | tf_op jit(solution)/shard_map/div | solution.py:55
  (188 shorter events, 108.7 us)
Async XLA Ops:
  7.2 137.9 %reduce-scatter.2.cloned.1.call-start = ((), (), s32[]{:S(2)}) async-start(), calls=%async_computation.1 | async-start | bytes 6291456 | tf_op jit(solution)/shard_map/reduce_scatter | solution.py:49
  87.9 95.5 %all-reduce.6.cloned.1.call-start = ((), (), s32[]{:S(2)}) async-start(), calls=%async_computation.2 | async-start | bytes 524288 | tf_op jit(solution)/shard_map/psum | solution.py:14
  147.5 276.0 %all-reduce.8.cloned.1.call-start = ((), (), s32[]{:S(2)}) async-start(), calls=%async_computation.3 | async-start | bytes 35651584 | tf_op jit(solution)/shard_map/psum | solution.py:54
  147.7 46.5 %copy-start.1 = (s32[1024]{0:T(1024)S(1)}, s32[1024]{0:T(1024)}, u32[]{:S(2)}) copy-start(s32[1024]{0:T(1024)} %param.10) | copy-start | bytes 12292
  147.8 46.5 %copy-start.2 = (f32[3]{0:T(128)S(1)}, f32[3]{0:T(128)}, u32[]{:S(2)}) copy-start(f32[3]{0:T(128)} %param.11) | copy-start | bytes 40
  183.4 9.5 %copy-start = (bf16[128,1024]{0,1:T(8,128)(2,1)S(1)}, bf16[128,1024]{0,1:T(8,128)(2,1)}, u32[]{:S(2)}) copy-start(bf16[128,1024]{0,1:T(8,128)(2,1)} %all-reduce.6.cloned.1.call-done) | copy-start | bytes 786436
  425.1 91.4 %all-reduce.10.cloned.1.call-start = ((), (), s32[]{:S(2)}) async-start(), calls=%async_computation.4 | async-start | bytes 2097152 | tf_op jit(solution)/shard_map/while/body/eval_jaxpr/psum | solution.py:14
  545.4 90.8 %all-reduce.10.cloned.1.call-start = ((), (), s32[]{:S(2)}) async-start(), calls=%async_computation.4 | async-start | bytes 2097152 | tf_op jit(solution)/shard_map/while/body/eval_jaxpr/psum | solution.py:14
  665.2 90.8 %all-reduce.10.cloned.1.call-start = ((), (), s32[]{:S(2)}) async-start(), calls=%async_computation.4 | async-start | bytes 2097152 | tf_op jit(solution)/shard_map/while/body/eval_jaxpr/psum | solution.py:14
  784.9 90.8 %all-reduce.10.cloned.1.call-start = ((), (), s32[]{:S(2)}) async-start(), calls=%async_computation.4 | async-start | bytes 2097152 | tf_op jit(solution)/shard_map/while/body/eval_jaxpr/psum | solution.py:14
Sparse Core Ops, SparseCore 0:
  88.0 56.9 reduce-scatter.1
  148.1 35.2 all-reduce.5
  194.4 229.1 all-reduce.7
  464.6 51.8 all-reduce.9
  584.9 51.1 all-reduce.9
  704.7 51.1 all-reduce.9
  824.4 51.1 all-reduce.9
where the time goes:
time: 926 us; the launch traced here: 925 us
  waiting for transfers between devices  528 us (57%)
  other arithmetic  239 us (26%)
  matrix products  117 us (13%)
  local copies, waits for them, and re-layouts  20.5 us (2%)
  between operations  14.1 us (2%)
    psum x5, waiting for transfers between devices, broadcast(): return lax.psum(jnp.where(mine, x, jnp.zeros_like(x)), axis)  242 us
    psum x1, waiting for transfers between devices, local(): gram_total, diag_total = lax.psum((gram_part, diag_part), ('tm', 'slope'))  229 us
    another operation x24, other arithmetic, step(): diag_factor = jnp.linalg.cholesky(jnp.where(act_pos == k, schur, identity))  136 us
    dot_general x3, matrix products, contract_rows(): lax.dot_general(left, right, (((0,), (0,)), ((), ())), preferred_element_...  91.4 us
    another operation x12, other arithmetic, step(): lax.linalg.triangular_solve(pivot, rest, left_side=False, lower=True, tra...  82.6 us
    reduce_scatter x1, waiting for transfers between devices, local(): lax.psum_scatter(contract_rows(frames, weights), 'tm', scatter_dimension=...  57.1 us
    dot_general x8, matrix products, exact_dot(): jnp.dot(left, right, precision=lax.Precision.HIGHEST, preferred_element_t...  19.4 us
  transfers between devices with their start and end apart: 7, of which 7 were waited for; matrix products, arithmetic and copies ran while one was open for 0% of the time, Pallas kernels for 0%

commit v1 on v0

v1 whole, which is shorter than its diff:
```python
import functools
import math

import jax
import jax.numpy as jnp
from jax import lax
from jax.experimental import pallas as pl
from jax.experimental.pallas import tpu as pltpu
from jax.sharding import PartitionSpec as P

PW = 1024
NDM = 3
F32 = jnp.float32
BF16 = jnp.bfloat16
LO = 256
B = 128
HIGHEST = lax.Precision.HIGHEST


def parity_bits(values):
    for shift_by in (16, 8, 4, 2, 1):
        values = jnp.bitwise_xor(values, jnp.right_shift(values, shift_by))
    return jnp.bitwise_and(values, 1)


def demod_kernel(codes, sgn, x_ref, w_ref, o_ref, had, tab, *, n_hi, n_top, group):
    i = pl.program_id(0)
    s = x_ref.shape[1]
    per = x_ref.shape[0] // LO

    @pl.when(i == 0)
    def _():
        r = lax.broadcasted_iota(jnp.int32, (LO, LO), 0)
        c = lax.broadcasted_iota(jnp.int32, (LO, LO), 1)
        had[...] = (1 - 2 * parity_bits(r & c)).astype(F32)

    for k in range(per):
        weights = (had[...] * w_ref[k : k + 1, :]).astype(BF16)
        tab[pl.ds(i * per + k, 1)] = jnp.dot(
            weights, x_ref[k * LO : (k + 1) * LO, :], preferred_element_type=F32
        )[None]

    @pl.when(i == pl.num_programs(0) - 1)
    def _():
        def column(t, _):
            rows = pl.ds(pl.multiple_of(t * 8, 8), 8)
            for l in range(s // 128):
                lanes = slice(l * 128, (l + 1) * 128)
                v = [tab[h, rows, lanes] for h in range(n_hi)]
                step = 1
                while step < n_hi:
                    for a in range(n_hi):
                        if not a & step:
                            v[a], v[a + step] = v[a] + v[a + step], v[a] - v[a + step]
                    step *= 2
                for h in range(n_hi):
                    tab[h, rows, lanes] = v[h]
                    for j in range(1, n_top):
                        tab[j * n_hi + h, rows, lanes] = v[h] * sgn[j]
            return 0

        lax.fori_loop(0, LO // 8, column, 0)
        flat = tab.reshape(n_top * n_hi * LO, s)

        def gather(t, _):
            base = pl.multiple_of(t * group, group)
            rows = [flat[pl.ds(codes[base + m], 1), :] for m in range(group)]
            o_ref[pl.ds(base, group), :] = jnp.concatenate(rows, axis=0).astype(BF16)
            return 0

        lax.fori_loop(0, o_ref.shape[0] // group, gather, 0)


def demod(frames, scale_rows, codes, sgn, per=8, group=16):
    f, s = frames.shape
    n = codes.shape[0]
    n_hi = f // LO
    n_top = sgn.shape[0]
    return pl.pallas_call(
        functools.partial(demod_kernel, n_hi=n_hi, n_top=n_top, group=group),
        out_shape=jax.ShapeDtypeStruct((n, s), BF16),
        grid_spec=pltpu.PrefetchScalarGridSpec(
            num_scalar_prefetch=2,
            grid=(n_hi // per,),
            in_specs=[
                pl.BlockSpec((per * LO, s), lambda i, *_: (i, 0)),
                pl.BlockSpec((per, LO), lambda i, *_: (i, 0)),
            ],
            out_specs=pl.BlockSpec((n, s), lambda i, *_: (0, 0)),
            scratch_shapes=[
                pltpu.VMEM((LO, LO), F32),
                pltpu.VMEM((n_top * n_hi, LO, s), F32),
            ],
        ),
        cost_estimate=pl.CostEstimate(
            flops=2 * f * LO * s, bytes_accessed=2 * f * s + 2 * n * s, transcendentals=0
        ),
        compiler_params=pltpu.CompilerParams(
            vmem_limit_bytes=40 << 20, dimension_semantics=("arbitrary",)
        ),
    )(codes, sgn, frames, scale_rows)


def across(v, lane):
    return jnp.broadcast_to(v[:, lane : lane + 1], (8, 128))


def down(v, row):
    return jnp.broadcast_to(v[row : row + 1, :], (8, 128))


def factor_tile(tile):
    lanes = lax.broadcasted_iota(jnp.int32, (8, 128), 1)
    subs = lax.broadcasted_iota(jnp.int32, (8, 128), 0)
    n = B // 8
    m = [tile[8 * g : 8 * g + 8, :] for g in range(n)]
    e = [jnp.where(lanes == subs + 8 * g, 1.0, 0.0).astype(F32) for g in range(n)]
    upper, inverse = [], []
    for q in range(n):
        cols = [across(m[q], 8 * q + j) for j in range(8)]
        s = {(i, j): down(cols[j], i) for j in range(8) for i in range(j, 8)}
        r = [down(m[q], i) for i in range(8)]
        t = [down(e[q], i) for i in range(8)]
        if q + 1 < n:
            c = [across(m[q + 1], 8 * q + j) for j in range(8)]
            m_next, e_next = m[q + 1], e[q + 1]
        far = {g: [across(m[g], 8 * q + j) for j in range(8)] for g in range(q + 2, n)}
        inv, u, w = [], [], []
        for j in range(8):
            root = lax.rsqrt(s[j, j])
            inv.append(root)
            l = {i: s[i, j] * root for i in range(j + 1, 8)}
            for i in range(j + 1, 8):
                for k in range(j + 1, i + 1):
                    s[i, k] = s[i, k] - l[i] * l[k]
                s[i, j] = l[i]
            u.append(r[j] * root)
            w.append(t[j] * root)
            for i in range(j + 1, 8):
                r[i] = r[i] - l[i] * u[j]
                t[i] = t[i] - l[i] * w[j]
            if q + 1 < n:
                lb = c[j] * root
                for k in range(j + 1, 8):
                    c[k] = c[k] - lb * l[k]
                m_next = m_next - lb * u[j]
                e_next = e_next - lb * w[j]
        u_rows, w_rows = u[0], w[0]
        for j in range(1, 8):
            u_rows = jnp.where(subs == j, u[j], u_rows)
            w_rows = jnp.where(subs == j, w[j], w_rows)
        upper.append(jnp.where(lanes >= subs + 8 * q, u_rows, 0.0))
        inverse.append(w_rows)
        if q + 1 < n:
            m[q + 1], e[q + 1] = m_next, e_next
        if q + 2 < n:
            ug, wg = [None] * 8, [None] * 8
            for j in reversed(range(8)):
                a, b = u[j], w[j]
                for i in range(j + 1, 8):
                    a = a - s[i, j] * ug[i]
                    b = b - s[i, j] * wg[i]
                ug[j], wg[j] = a * inv[j], b * inv[j]
            for g in range(q + 2, n):
                for j in range(8):
                    m[g] = m[g] - far[g][j] * ug[j]
                    e[g] = e[g] - far[g][j] * wg[j]
    return upper, inverse


def factor_kernel(pos, *refs, n_slope, total_rows, block):
    pieces = refs[:n_slope]
    load_ref, o_ref, panel, u_ref, inverse, rows = refs[n_slope:]
    width = pieces[0].shape[0]
    s_dev = pieces[0].shape[1]
    for j in range(n_slope):
        at = pl.multiple_of(pos[1 + j] * s_dev, s_dev)
        panel[:, pl.ds(at, s_dev)] = pieces[j][...]
    gram = lax.dot_general(
        panel[...], panel[...], (((1,), (1,)), ((), ())), preferred_element_type=F32
    )
    r = lax.broadcasted_iota(jnp.int32, (width, width), 0)
    c = lax.broadcasted_iota(jnp.int32, (width, width), 1)
    u_ref[...] = gram / float(total_rows) + jnp.where(r == c, load_ref[...], 0.0)
    n_blocks = width // B

    def body(k, _):
        o = pl.multiple_of(k * B, B)
        upper, inv = factor_tile(u_ref[pl.ds(o, B), pl.ds(o, B)])
        for g in range(B // 8):
            u_ref[pl.ds(o + 8 * g, 8), pl.ds(o, B)] = upper[g]
            inverse[8 * g : 8 * g + 8, :] = inv[g]
        for kk in range(n_blocks - 1):

            @pl.when(k == kk)
            def _():
                r0 = (kk + 1) * B
                strip = jnp.dot(
                    inverse[...], u_ref[kk * B : r0, r0:], precision=HIGHEST, preferred_element_type=F32
                )
                u_ref[kk * B : r0, r0:] = strip
                u_ref[r0:, r0:] = u_ref[r0:, r0:] - lax.dot_general(
                    strip, strip, (((0,), (0,)), ((), ())), precision=HIGHEST, preferred_element_type=F32
                )

        return 0

    lax.fori_loop(0, n_blocks, body, 0)
    wide = rows.shape[0]
    first = pos[0] * block
    base = first // wide * wide
    rows[...] = u_ref[:, pl.ds(pl.multiple_of(base, wide), wide)].T
    own = rows[pl.ds(pl.multiple_of(first - base, 8), block), :]
    row_ids = first + lax.broadcasted_iota(jnp.int32, (block, width), 0)
    col_ids = lax.broadcasted_iota(jnp.int32, (block, width), 1)
    o_ref[...] = jnp.where(row_ids >= col_ids, own, 0.0)


def factor_rows(pieces, load_col, pos, block, total_rows):
    n_slope = len(pieces)
    width, s_dev = pieces[0].shape
    vmem = pl.BlockSpec(memory_space=pltpu.VMEM)
    return pl.pallas_call(
        functools.partial(factor_kernel, n_slope=n_slope, total_rows=total_rows, block=block),
        out_shape=jax.ShapeDtypeStruct((block, width), F32),
        in_specs=[pl.BlockSpec(memory_space=pltpu.SMEM)] + [vmem] * (n_slope + 1),
        out_specs=vmem,
        scratch_shapes=[
            pltpu.VMEM((width, n_slope * s_dev), BF16),
            pltpu.VMEM((width, width), F32),
            pltpu.VMEM((B, B), F32),
            pltpu.VMEM((max(block, 128), width), F32),
        ],
        cost_estimate=pl.CostEstimate(
            flops=2 * width * width * total_rows * 10, bytes_accessed=140 << 20, transcendentals=width
        ),
        compiler_params=pltpu.CompilerParams(vmem_limit_bytes=40 << 20),
    )(pos, *pieces, load_col)


def gram_kernel(pos, *refs, n_slope, total_rows):
    rows_in = refs[:n_slope]
    panel_in = refs[n_slope : 2 * n_slope]
    o_ref, left, right = refs[2 * n_slope :]
    s_dev = rows_in[0].shape[1]

    @pl.when(pl.program_id(0) == 0)
    def _():
        for j in range(n_slope):
            at = pl.multiple_of(pos[1 + j] * s_dev, s_dev)
            right[pl.ds(at, s_dev), :] = panel_in[j][...].T

    for j in range(n_slope):
        at = pl.multiple_of(pos[1 + j] * s_dev, s_dev)
        left[:, pl.ds(at, s_dev)] = rows_in[j][...]
    o_ref[...] = jnp.dot(left[...], right[...], preferred_element_type=F32) / float(total_rows)


def gram_rows(pieces, panel, pos, total_rows, tile=256):
    n_slope = len(pieces)
    n, s_dev = pieces[0].shape
    width = panel[0].shape[0]
    return pl.pallas_call(
        functools.partial(gram_kernel, n_slope=n_slope, total_rows=total_rows),
        out_shape=jax.ShapeDtypeStruct((n, width), F32),
        grid_spec=pltpu.PrefetchScalarGridSpec(
            num_scalar_prefetch=1,
            grid=(n // tile,),
            in_specs=[pl.BlockSpec((tile, s_dev), lambda i, *_: (i, 0))] * n_slope
            + [pl.BlockSpec((width, s_dev), lambda i, *_: (0, 0))] * n_slope,
            out_specs=pl.BlockSpec((tile, width), lambda i, *_: (i, 0)),
            scratch_shapes=[
                pltpu.VMEM((tile, n_slope * s_dev), BF16),
                pltpu.VMEM((n_slope * s_dev, width), BF16),
            ],
        ),
        cost_estimate=pl.CostEstimate(
            flops=2 * n * width * total_rows, bytes_accessed=4 * n * width + 2 * n * total_rows, transcendentals=0
        ),
        compiler_params=pltpu.CompilerParams(
            vmem_limit_bytes=40 << 20, dimension_semantics=("arbitrary",)
        ),
    )(pos, *pieces, *panel)


def local(frames, frame_scale, codes, assign, loads):
    f_dev, s_dev = frames.shape
    n_tm, n_slope, n_act = lax.axis_size("tm"), lax.axis_size("slope"), lax.axis_size("act")
    tm_pos, slope_pos, act_pos = lax.axis_index("tm"), lax.axis_index("slope"), lax.axis_index("act")
    total_frames = f_dev * n_tm
    total_rows = s_dev * n_slope
    block = PW // n_act
    n_y = n_slope // 2

    own_codes = codes[:PW]
    panel_codes = own_codes
    for r in range(1, n_act):
        sent = lax.ppermute(own_codes, "act", [(0, r)])
        panel_codes = jnp.where(act_pos == r, sent, panel_codes)
    scale_rows = frame_scale.astype(BF16).astype(F32).reshape(f_dev // LO, LO)
    sgn = (1 - 2 * parity_bits(lax.iota(jnp.int32, n_tm) & tm_pos)).astype(F32)

    def sum_tm(part):
        total = part.astype(F32)
        for r in range(1, n_tm):
            total = total + lax.ppermute(
                part, "tm", [(i, (i + r) % n_tm) for i in range(n_tm)]
            ).astype(F32)
        return (total * (1.0 / math.sqrt(total_frames))).astype(BF16)

    def gather_slopes(im):
        column = [im]
        for r in range(1, n_y):
            column.append(
                lax.ppermute(
                    im,
                    "slope",
                    [(2 * y + k, 2 * ((y + r) % n_y) + k) for y in range(n_y) for k in range(2)],
                )
            )
        swap = [(i, i ^ 1) for i in range(n_slope)]
        return column + [lax.ppermute(v, "slope", swap) for v in column]

    y_pos, core_pos = slope_pos // 2, slope_pos % 2
    origin = [(y_pos - r + n_y) % n_y for r in range(n_y)]
    pos = jnp.stack(
        [act_pos] + [2 * y + core_pos for y in origin] + [2 * y + 1 - core_pos for y in origin]
    ).astype(jnp.int32)

    panel = gather_slopes(sum_tm(demod(frames, scale_rows, panel_codes, sgn)))
    mine = gather_slopes(sum_tm(demod(frames, scale_rows, codes, sgn)))

    mirror_ids = lax.broadcasted_iota(jnp.int32, (NDM, PW), 0)
    load_col = jnp.sum(jnp.where(assign[None, :] == mirror_ids, loads[:, None], 0.0), axis=0)
    factor = factor_rows(panel, load_col[None, :], pos, block, total_rows)
    gram_panel = gram_rows(mine, panel, pos, total_rows)
    return (gram_panel, factor)


def solution(mesh):
    return jax.shard_map(
        local,
        mesh=mesh,
        in_specs=(P("tm", "slope"), P("tm"), P("act"), P(), P()),
        out_specs=(P("act", None), P("act", None)),
        check_vma=False,
    )
```

time: 926 us -> 199 us (0.21)
  waiting for transfers between devices: 528 us -> 82 us
  other arithmetic: 239 us -> 2.47 us
  matrix products: 117 us -> 0 us
  Pallas kernels: 0 us -> 92.7 us
  local copies, waits for them, and re-layouts: 20.5 us -> 5.19 us
  starting transfers between devices: 0.47 us -> 15.6 us
  between operations: 14.1 us -> 0.74 us
    psum x6 -> x0, waiting for transfers between devices: 471 us -> none  [the longest x5 242 us: broadcast(): return lax.psum(jnp.where(mine, x, jnp.zeros_like(x)), axis)]
    another operation x36 -> x0, other arithmetic: 218 us -> none  [the longest x24 136 us: step(): diag_factor = jnp.linalg.cholesky(jnp.where(act_pos == k, schur, identity))]
    dot_general x11 -> x0, matrix products: 111 us -> none  [the longest x3 91.4 us: contract_rows(): lax.dot_general(left, right, (((0,), (0,)), ((), ())), preferred_element_...]
    pallas_call x0 -> x4, Pallas kernels: none -> 92.7 us  [the longest x1 52 us: factor_rows(): pl.pallas_call(functools.partial(factor_kernel, n_slope=n_slope, total_ro...]
    ppermute x0 -> x11, waiting for transfers between devices: none -> 82 us  [the longest x2 55.8 us: sum_tm(): lax.ppermute(part, 'tm', [(i, (i + r) % n_tm) for i in range(n_tm)])]
    reduce_scatter x1 -> x0, waiting for transfers between devices: 57.1 us -> none  [local(): lax.psum_scatter(contract_rows(frames, weights), 'tm', scatter_dimension=...]
    another operation x73 -> x1, local copies, waits for them, and re-layouts: 18 us -> 0.08 us  [local(): jnp.stack([act_pos] + [2 * y + core_pos for y in origin] + [2 * y + 1 - c...]
    ppermute x0 -> x11, starting transfers between devices: none -> 15.6 us  [the longest x3 8.07 us: local(): sent = lax.ppermute(own_codes, 'act', [(0, r)])]
  transfers between devices with their start and end apart: 7 -> 11, of which waited for: 7 -> 5; matrix products, arithmetic and copies ran while one was open for 0% -> 1% of each run, Pallas kernels for 0% -> 30%
where the time goes in v1:
time: 199 us
  Pallas kernels  92.7 us (47%)
  waiting for transfers between devices  82 us (41%)
  starting transfers between devices  15.6 us (8%)
  local copies, waits for them, and re-layouts  5.19 us (3%)
  other arithmetic  2.47 us (1%)
    ppermute x2, waiting for transfers between devices, sum_tm(): lax.ppermute(part, 'tm', [(i, (i + r) % n_tm) for i in range(n_tm)])  55.8 us
    pallas_call x1, Pallas kernels, factor_rows(): pl.pallas_call(functools.partial(factor_kernel, n_slope=n_slope, total_ro...  52 us
    ppermute x2, waiting for transfers between devices, gather_slopes(): lax.ppermute(im, 'slope', [(2 * y + k, 2 * ((y + r) % n_y) + k) for y in...  23.6 us
    pallas_call x2, Pallas kernels, demod(): pl.pallas_call(functools.partial(demod_kernel, n_hi=n_hi, n_top=n_top, gr...  22.5 us
    pallas_call x1, Pallas kernels, gram_rows(): pl.pallas_call(functools.partial(gram_kernel, n_slope=n_slope, total_rows...  18.2 us
    ppermute x3, starting transfers between devices, local(): sent = lax.ppermute(own_codes, 'act', [(0, r)])  8.07 us
    unnamed x10, local copies, waits for them, and re-layouts  5.09 us
    ppermute x2, starting transfers between devices, sum_tm(): lax.ppermute(part, 'tm', [(i, (i + r) % n_tm) for i in range(n_tm)])  4.56 us
  transfers between devices with their start and end apart: 11, of which 5 were waited for; matrix products, arithmetic and copies ran while one was open for 1% of the time, Pallas kernels for 30%

profile of v1, /device:TPU:0, one launch (start us, length us, event | category | flops | bytes accessed | tf_op | source)
XLA Modules:
  0.0 198.7 jit_solution(13704302519542714073)
XLA Ops:
  0.7 0.8 convert_convert_fusion
  1.4 2.2 %copy-done = bf16[8192,256]{1,0:T(8,128)(2,1)S(1)} copy-done((bf16[8192,256]{1,0:T(8,128)(2,1)S(1)}, bf16[8192,256]{1,0:T(8,128)(2,1)}, u32[]{:S(2)}) %copy-start) | copy-done | bytes 4194328
  3.6 0.7 copy-done.2
  4.3 14.6 %shard_map.68 = bf16[4096,256]{1,0:T(8,128)(2,1)S(1)} custom-call(s32[4096]{0:T(1024)S(1)} %copy-done.2, f32[2]{0:T(128)S(1)} %fusion.3.sgn, bf16[8192,256]{1,0:T(8,128)(2,1)S(1)} %copy-done, f32[32,256]{1,0:T(8,128)S(1)} %reshape.14.w_ref), custom_call_target="tpu_custom_call" | custom-call | flops 1073741824 | bytes 6291456 | tf_op jit(solution)/shard_map/pallas_call | solution.py:79
  18.9 3.0 %collective-permute-start = (bf16[4096,256]{1,0:T(8,128)(2,1)S(1)}, bf16[4096,256]{1,0:T(8,128)(2,1)S(1)}, u32[]{:S(2)}, u32[]{:S(2)}) collective-permute-start(bf16[4096,256]{1,0:T(8,128)(2,1)S(1)} %shard_map.68), channel_id=1, source_target_pairs={{0,16},{16,0},{1,17},{17,1},{2,18},{18,2},{3,19},{19,3},{4,20},{20... | collective-permute-start | bytes 6291464 | tf_op jit(solution)/shard_map/ppermute | solution.py:306
  21.9 45.6 %collective-permute-done = bf16[4096,256]{1,0:T(8,128)(2,1)S(1)} collective-permute-done((bf16[4096,256]{1,0:T(8,128)(2,1)S(1)}, bf16[4096,256]{1,0:T(8,128)(2,1)S(1)}, u32[]{:S(2)}, u32[]{:S(2)}) %collective-permute-start) | collective-permute-done | bytes 2097184 | tf_op jit(solution)/shard_map/ppermute | solution.py:306
  67.5 0.7 multiply_convert_fusion.refs_0_
  68.3 1.8 collective-permute-start.1
  70.1 5.5 %collective-permute-start.4 = (s32[1024]{0:T(1024)S(1)}, s32[1024]{0:T(1024)S(1)}, u32[]{:S(2)}, u32[]{:S(2)}) collective-permute-start(s32[1024]{0:T(1024)S(1)} %slice.3), channel_id=1, source_target_pairs={{0,3},{4,7},{8,11},{12,15},{16,19},{20,23},{24,27},{28,31}} | collective-permute-start | bytes 12296 | tf_op jit(solution)/shard_map/ppermute | solution.py:298
  75.6 1.3 collective-permute-start.5
  76.9 1.3 collective-permute-start.6
  78.3 1.3 collective-permute-done.6
  79.5 0.7 select_select_fusion.codes
  80.2 2.2 %copy-done.1 = bf16[8192,256]{1,0:T(8,128)(2,1)S(1)} copy-done((bf16[8192,256]{1,0:T(8,128)(2,1)S(1)}, bf16[8192,256]{1,0:T(8,128)(2,1)}, u32[]{:S(2)}) %copy-start.1) | copy-done | bytes 4194328
  82.4 7.9 %shard_map.69 = bf16[1024,256]{1,0:T(8,128)(2,1)S(1)} custom-call(s32[1024]{0:T(1024)S(1)} %select_select_fusion.codes, f32[2]{0:T(128)S(1)} %fusion.3.sgn, bf16[8192,256]{1,0:T(8,128)(2,1)S(1)} %copy-done.1, f32[32,256]{1,0:T(8,128)S(1)} %reshape.14.w_ref), custom_call_target="tpu_custom_call" | custom-call | flops 1073741824 | bytes 4718592 | tf_op jit(solution)/shard_map/pallas_call | solution.py:79
  90.3 1.6 collective-permute-start.7
  91.9 10.2 %collective-permute-done.7 = bf16[1024,256]{1,0:T(8,128)(2,1)S(1)} collective-permute-done((bf16[1024,256]{1,0:T(8,128)(2,1)S(1)}, bf16[1024,256]{1,0:T(8,128)(2,1)S(1)}, u32[]{:S(2)}, u32[]{:S(2)}) %collective-permute-start.7) | collective-permute-done | bytes 524320 | tf_op jit(solution)/shard_map/ppermute | solution.py:306
  102.0 0.2 multiply_convert_fusion.1.refs_4_.refs_0_
  102.2 0.6 collective-permute-start.8
  102.8 23.6 %collective-permute-done.8.refs_5_.refs_1_ = bf16[1024,256]{1,0:T(8,128)(2,1)S(1)} collective-permute-done((bf16[1024,256]{1,0:T(8,128)(2,1)S(1)}, bf16[1024,256]{1,0:T(8,128)(2,1)S(1)}, u32[]{:S(2)}, u32[]{:S(2)}) %collective-permute-start.8) | collective-permute-done | bytes 524320 | tf_op jit(solution)/shard_map/ppermute | solution.py:315
  126.5 0.5 collective-permute-start.2
  127.2 1.3 collective-permute-done.10.refs_7_.refs_3_
  128.4 52.0 %shard_map.71 = f32[256,1024]{1,0:T(8,128)} custom-call(s32[5]{0:T(128)S(1)} %stack.23.pos, bf16[1024,256]{1,0:T(8,128)(2,1)S(1)} %multiply_convert_fusion.1.refs_4_.refs_0_, bf16[1024,256]{1,0:T(8,128)(2,1)S(1)} %collective-permute-done.8.refs_5_.refs_1_, bf16[1024,256]{1,0:T(8,128)(2,1)} %collective-permute-done.9.refs_6_.refs_2_, ...), custom_call_target="tpu_custom_call" | custom-call | flops 21474836480 | bytes 146800640 | tf_op jit(solution)/shard_map/pallas_call | solution.py:223
  180.5 18.2 %shard_map.70 = f32[4096,1024]{1,0:T(8,128)} custom-call(s32[5]{0:T(128)S(1)} %stack.23.pos, bf16[4096,256]{1,0:T(8,128)(2,1)S(1)} %multiply_convert_fusion.refs_0_, bf16[4096,256]{1,0:T(8,128)(2,1)} %collective-permute-done.1.refs_1_, bf16[4096,256]{1,0:T(8,128)(2,1)S(1)} %collective-permute-done.2.refs_2_, ...), custom_call_target="tpu_custom_call" | custom-call | flops 8589934592 | bytes 25165824 | tf_op jit(solution)/shard_map/pallas_call | solution.py:263
  (21 shorter events, 0.3 us)
Async XLA Ops:
  1.4 2.2 %copy-start = (bf16[8192,256]{1,0:T(8,128)(2,1)S(1)}, bf16[8192,256]{1,0:T(8,128)(2,1)}, u32[]{:S(2)}) copy-start(bf16[8192,256]{1,0:T(8,128)(2,1)} %x_ref.3) | copy-start | bytes 12582916
  3.6 0.7 copy-start.2
  18.9 48.6 %collective-permute-start = (bf16[4096,256]{1,0:T(8,128)(2,1)S(1)}, bf16[4096,256]{1,0:T(8,128)(2,1)S(1)}, u32[]{:S(2)}, u32[]{:S(2)}) collective-permute-start(bf16[4096,256]{1,0:T(8,128)(2,1)S(1)} %shard_map.68), channel_id=1, source_target_pairs={{0,16},{16,0},{1,17},{17,1},{2,18},{18,2},{3,19},{19,3},{4,20},{20... | collective-permute-start | bytes 6291464 | tf_op jit(solution)/shard_map/ppermute | solution.py:306
  68.3 58.7 %collective-permute-start.1 = (bf16[4096,256]{1,0:T(8,128)(2,1)S(1)}, bf16[4096,256]{1,0:T(8,128)(2,1)}, u32[]{:S(2)}, u32[]{:S(2)}) collective-permute-start(bf16[4096,256]{1,0:T(8,128)(2,1)S(1)} %multiply_convert_fusion.refs_0_), channel_id=1, source_target_pairs={{0,8},{4,12},{8,0},{12,4},{1,9},{5,13},{9,1},{13,5},{2,10},{6,14},... | collective-permute-start | bytes 6291464 | tf_op jit(solution)/shard_map/ppermute | solution.py:315
  70.1 8.1 %collective-permute-start.4 = (s32[1024]{0:T(1024)S(1)}, s32[1024]{0:T(1024)S(1)}, u32[]{:S(2)}, u32[]{:S(2)}) collective-permute-start(s32[1024]{0:T(1024)S(1)} %slice.3), channel_id=1, source_target_pairs={{0,3},{4,7},{8,11},{12,15},{16,19},{20,23},{24,27},{28,31}} | collective-permute-start | bytes 12296 | tf_op jit(solution)/shard_map/ppermute | solution.py:298
  75.6 2.6 %collective-permute-start.5 = (s32[1024]{0:T(1024)S(1)}, s32[1024]{0:T(1024)S(1)}, u32[]{:S(2)}, u32[]{:S(2)}) collective-permute-start(s32[1024]{0:T(1024)S(1)} %slice.3), channel_id=1, source_target_pairs={{0,2},{4,6},{8,10},{12,14},{16,18},{20,22},{24,26},{28,30}} | collective-permute-start | bytes 12296 | tf_op jit(solution)/shard_map/ppermute | solution.py:298
  76.9 2.6 %collective-permute-start.6 = (s32[1024]{0:T(1024)S(1)}, s32[1024]{0:T(1024)S(1)}, u32[]{:S(2)}, u32[]{:S(2)}) collective-permute-start(s32[1024]{0:T(1024)S(1)} %slice.3), channel_id=1, source_target_pairs={{0,1},{4,5},{8,9},{12,13},{16,17},{20,21},{24,25},{28,29}} | collective-permute-start | bytes 12296 | tf_op jit(solution)/shard_map/ppermute | solution.py:298
  80.2 2.2 %copy-start.1 = (bf16[8192,256]{1,0:T(8,128)(2,1)S(1)}, bf16[8192,256]{1,0:T(8,128)(2,1)}, u32[]{:S(2)}) copy-start(bf16[8192,256]{1,0:T(8,128)(2,1)} %x_ref.3) | copy-start | bytes 12582916
  82.4 44.7 %copy-start.3 = (s32[1024]{0:T(1024)S(1)}, s32[1024]{0:T(1024)}, u32[]{:S(2)}) copy-start(s32[1024]{0:T(1024)} %param.8) | copy-start | bytes 12292
  82.4 44.7 %copy-start.4 = (f32[3]{0:T(128)S(1)}, f32[3]{0:T(128)}, u32[]{:S(2)}) copy-start(f32[3]{0:T(128)} %param.9) | copy-start | bytes 40
  90.3 11.7 %collective-permute-start.7 = (bf16[1024,256]{1,0:T(8,128)(2,1)S(1)}, bf16[1024,256]{1,0:T(8,128)(2,1)S(1)}, u32[]{:S(2)}, u32[]{:S(2)}) collective-permute-start(bf16[1024,256]{1,0:T(8,128)(2,1)S(1)} %shard_map.69), channel_id=1, source_target_pairs={{0,16},{16,0},{1,17},{17,1},{2,18},{18,2},{3,19},{19,3},{4,20},{20... | collective-permute-start | bytes 1572872 | tf_op jit(solution)/shard_map/ppermute | solution.py:306
  102.2 24.2 %collective-permute-start.8 = (bf16[1024,256]{1,0:T(8,128)(2,1)S(1)}, bf16[1024,256]{1,0:T(8,128)(2,1)S(1)}, u32[]{:S(2)}, u32[]{:S(2)}) collective-permute-start(bf16[1024,256]{1,0:T(8,128)(2,1)S(1)} %multiply_convert_fusion.1.refs_4_.refs_0_), channel_id=1, source_target_pairs={{0,8},{4,12},{8,0},{12,4},{1,9},{5,13},{9,1},{13,5},{2,10},{6,14},... | collective-permute-start | bytes 1572872 | tf_op jit(solution)/shard_map/ppermute | solution.py:315
  102.8 24.4 %collective-permute-start.9 = (bf16[1024,256]{1,0:T(8,128)(2,1)S(1)}, bf16[1024,256]{1,0:T(8,128)(2,1)}, u32[]{:S(2)}, u32[]{:S(2)}) collective-permute-start(bf16[1024,256]{1,0:T(8,128)(2,1)S(1)} %multiply_convert_fusion.1.refs_4_.refs_0_), channel_id=1, source_target_pairs={{0,4},{4,0},{8,12},{12,8},{1,5},{5,1},{9,13},{13,9},{2,6},{6,2},{1... | collective-permute-start | bytes 1572872 | tf_op jit(solution)/shard_map/ppermute | solution.py:322
  126.4 2.0 %collective-permute-start.10 = (bf16[1024,256]{1,0:T(8,128)(2,1)S(1)}, bf16[1024,256]{1,0:T(8,128)(2,1)}, u32[]{:S(2)}, u32[]{:S(2)}) collective-permute-start(bf16[1024,256]{1,0:T(8,128)(2,1)S(1)} %collective-permute-done.8.refs_5_.refs_1_), channel_id=1, source_target_pairs={{0,4},{4,0},{8,12},{12,8},{1,5},{5,1},{9,13},{13,9},{2,6},{6,2},{1... | collective-permute-start | bytes 1572872 | tf_op jit(solution)/shard_map/ppermute | solution.py:322
  126.5 54.0 %collective-permute-start.2 = (bf16[4096,256]{1,0:T(8,128)(2,1)S(1)}, bf16[4096,256]{1,0:T(8,128)(2,1)S(1)}, u32[]{:S(2)}, u32[]{:S(2)}) collective-permute-start(bf16[4096,256]{1,0:T(8,128)(2,1)S(1)} %multiply_convert_fusion.refs_0_), channel_id=1, source_target_pairs={{0,4},{4,0},{8,12},{12,8},{1,5},{5,1},{9,13},{13,9},{2,6},{6,2},{1... | collective-permute-start | bytes 6291464 | tf_op jit(solution)/shard_map/ppermute | solution.py:322
  127.0 53.5 %collective-permute-start.3 = (bf16[4096,256]{1,0:T(8,128)(2,1)}, bf16[4096,256]{1,0:T(8,128)(2,1)S(1)}, u32[]{:S(2)}, u32[]{:S(2)}) collective-permute-start(bf16[4096,256]{1,0:T(8,128)(2,1)} %collective-permute-done.1.refs_1_), channel_id=1, source_target_pairs={{0,4},{4,0},{8,12},{12,8},{1,5},{5,1},{9,13},{13,9},{2,6},{6,2},{1... | collective-permute-start | bytes 6291464 | tf_op jit(solution)/shard_map/ppermute | solution.py:322
